TPU v7x, 32 devices: a whole 2x2x4 slice. The times are simulated.
32 devices in a mesh: grp: 2 (over y), ta: 4 (over z), gx: 4 (over x, core).
Axes of the slice: x: 2, y: 2, z: 4, core: 2. Of those that a mesh axis runs over, the one named last changes fastest.
Arguments:
- vectors: bfloat16 [8, 2, 3, 8192, 128], P(('grp', 'ta'), None, None, 'gx'), parts along dimension 0, may hold values from -6 to 6
- peramb: bfloat16 [8, 16, 2, 128, 128], P(('grp', 'ta')), parts along dimension 0, may hold values from -0.5 to 0.5
- momenta: int32 [8, 3], P('grp'), parts along dimension 0, may hold values from -2 to 2, as said below
- sink_mom: int32 [32], P('grp'), parts along dimension 0, may hold values from 0 to 3
- spin_pick: int32 [32], P('grp'), parts along dimension 0, may hold values from 0 to 15
- src_time: int32 [2], P('grp'), parts along dimension 0, may hold values from 0 to 65535
Outputs:
- corr: float32 [8, 16, 2, 128, 128], P(('grp', 'ta'), 'gx'), parts along dimension 0
There are 2 independent parts, one for each index of `grp`. A program takes and returns all parts, laid end to end along the dimension named above; each array names one. Nothing has to cross between parts.
Inputs may be any that keep to these rules, and one draw needn't show every extreme that they name: `momenta`: every component of every momentum is nonzero.
All inputs are finite; a program needn't handle non-finite values.
Results may differ from a plain program's by a relative error of at most 0.0038.
Values sent between devices are 32-bit elements; how exact they have to be, the bound alone decides.
No kernel may reach another device: no remote copies, remote signals or barrier semaphores. Data moves between devices by JAX's collectives and lax.ppermute only.
A program may use at most 64 MiB of HBM per device.

v0:
```python
import math

import jax
import jax.numpy as jnp
from jax import lax
from jax.sharding import PartitionSpec as P

RANK = 128
LY = 32
LZ = 32
NMOM = 4


def broadcast(array, axis, root):
    mine = lax.axis_index(axis) == root
    return lax.psum(jnp.where(mine, array, jnp.zeros_like(array)), axis)


def phase_angle(momentum, first_x, count, extent_x):
    site_ids = jnp.arange(count, dtype=jnp.int32)
    coord_x = first_x + site_ids // (LY * LZ)
    coord_y = site_ids // LZ % LY
    coord_z = site_ids % LZ
    part_x = jnp.mod(momentum[0] * coord_x, extent_x).astype(jnp.float32) / extent_x
    part_y = jnp.mod(momentum[1] * coord_y, LY).astype(jnp.float32) / LY
    part_z = jnp.mod(momentum[2] * coord_z, LZ).astype(jnp.float32) / LZ
    return 2.0 * math.pi * (part_x + part_y + part_z)


def elemental(vec_re, vec_im, angle, scale):
    cos_part = jnp.cos(angle)[None, :, None]
    sin_part = jnp.sin(angle)[None, :, None]
    real_f = vec_re.astype(jnp.float32)
    imag_f = vec_im.astype(jnp.float32)
    phased_re = real_f * cos_part + imag_f * sin_part
    phased_im = imag_f * cos_part - real_f * sin_part
    upper = jnp.concatenate([phased_re, phased_im], axis=-1)
    lower = jnp.concatenate([phased_im, -phased_re], axis=-1)
    phased = jnp.concatenate([upper, lower], axis=0).astype(jnp.bfloat16)
    total_rows = phased.shape[0] * phased.shape[1]
    phased = phased.reshape(total_rows, -1)
    stacked = jnp.concatenate([vec_re, vec_im], axis=0).reshape(total_rows, -1)
    product = (
        lax.dot_general(
            stacked, phased, (((0,), (0,)), ((), ())), preferred_element_type=jnp.float32
        )
        * scale
    )
    width = vec_re.shape[-1]
    return jnp.stack([product[:, :width], product[:, width:]])


def matmul_high(left, right):
    return jnp.matmul(left, right, precision=lax.Precision.HIGHEST)


def complex_mul(left, right):
    real_part = matmul_high(left[..., 0, :, :], right[..., 0, :, :]) - matmul_high(
        left[..., 1, :, :], right[..., 1, :, :]
    )
    imag_part = matmul_high(left[..., 0, :, :], right[..., 1, :, :]) + matmul_high(
        left[..., 1, :, :], right[..., 0, :, :]
    )
    return jnp.stack([real_part, imag_part], axis=-3)


def body(vectors, peramb, momenta, sink_mom, spin_pick, src_time):
    vec_re = vectors[0, 0]
    vec_im = vectors[0, 1]
    sites = vec_re.shape[1]
    slab_x = sites // (LY * LZ)
    groups = lax.axis_size("gx")
    extent_x = slab_x * groups
    first_x = lax.axis_index("gx") * slab_x
    scale = 1.0 / math.sqrt(vec_re.shape[0] * sites * groups)
    root_slice = jnp.mod(src_time[0], lax.axis_size("ta"))
    local_terms = jnp.stack(
        [
            elemental(vec_re, vec_im, phase_angle(momenta[m], first_x, sites, extent_x), scale)
            for m in range(NMOM)
        ]
    )
    row_sums = lax.psum_scatter(local_terms, "gx", scatter_dimension=2, tiled=True)
    source_part = broadcast(row_sums[0], "ta", root_slice)
    source = lax.all_gather(source_part, "gx", axis=1, tiled=True)
    chosen = peramb[0][spin_pick].astype(jnp.float32)
    sink_rows = complex_mul(row_sums[sink_mom], chosen)
    corr_rows = complex_mul(sink_rows, source) / math.sqrt(RANK)
    result = lax.all_to_all(corr_rows, "gx", split_axis=0, concat_axis=2, tiled=True)
    return result[None]


def solution(mesh):
    placed = (
        P(("grp", "ta"), None, None, "gx", None),
        P(("grp", "ta"), None, None, None, None),
        P("grp", None),
        P("grp"),
        P("grp"),
        P("grp"),
    )
    return jax.shard_map(
        body,
        mesh=mesh,
        in_specs=placed,
        out_specs=P(("grp", "ta"), "gx", None, None, None),
        check_vma=False,
    )
```

profile of v0, /device:TPU:0, one launch (start us, length us, event | category | flops | bytes accessed | tf_op | source)
XLA Modules:
  0.0 106.9 jit_solution(7913322950592608295)
XLA Ops:
  6.5 1.8 %fusion.156 = (s32[1,1]{1,0:T(1,128)}, s32[1,1]{1,0:T(1,128)}, s32[1,1]{1,0:T(1,128)}, s32[1,1]{1,0:T(1,128)}, s32[1,1]{1,0:T(1,128)}, /*index=5*/s32[1,1]{1,0:T...) fusion(s32[4,3]{1,0:T(4,128)} %param.8), kind=kLoop, calls=%fused_computation.241 | loop fusion | bytes 96 | tf_op jit(solution)/shard_map/slice | solution.py:24
  8.4 3.3 %slice_bitcast_fusion.1 = (bf16[3,2048,128]{2,1,0:T(8,128)(2,1)S(1)}, bf16[3,2048,128]{2,1,0:T(8,128)(2,1)}) fusion(bf16[1,2,3,2048,128]{4,3,2,1,0:T(8,128)(2,1)} %param.6), kind=kLoop, calls=%fused_computation.72 | loop fusion | bytes 6291456 | tf_op jit(solution)/shard_map/squeeze | solution.py:68
  11.6 1.9 %fusion.146 = (f32[2048]{0:T(1024)S(1)}, f32[2048]{0:T(1024)S(1)}) fusion(s32[]{:T(128)} %bitcast.18, s32[]{:T(128)} %bitcast.17, s32[]{:T(128)S(6)} %mul.324, s32[]{:T(128)} %bitcast.16), kind=kLoop, calls=%fused_computation.229 | loop fusion | flops 153600 | bytes 16400 | tf_op jit(solution)/shard_map/sin | solution.py:32
  13.5 2.0 %fusion.148 = (f32[2048]{0:T(1024)S(1)}, f32[2048]{0:T(1024)S(1)}) fusion(s32[]{:T(128)} %bitcast.11, s32[]{:T(128)} %bitcast.10, s32[]{:T(128)S(6)} %mul.324, s32[]{:T(128)} %bitcast.9), kind=kLoop, calls=%fused_computation.231 | loop fusion | flops 153600 | bytes 16400 | tf_op jit(solution)/shard_map/sin | solution.py:32
  15.5 4.9 %fusion.46 = (bf16[3,2048,128]{2,1,0:T(8,128)(2,1)S(1)}, bf16[3,2048,128]{2,1,0:T(8,128)(2,1)S(1)}, bf16[3,2048,128]{2,1,0:T(8,128)(2,1)S(1)}, bf16[3,2048,128]{...) fusion(f32[2048]{0:T(1024)S(1)} %get-tuple-element.51, ...), kind=kLoop, calls=%fused_computation.69 | loop fusion | flops 17301504 | bytes 12615680 | tf_op jit(solution)/shard_map/convert.16
  20.4 1.1 %fusion.65 = f32[128,256]{1,0:T(8,128)S(1)} fusion(bf16[3,2048,128]{2,1,0:T(8,128)(2,1)S(1)} %get-tuple-element.10, bf16[3,2048,128]{2,1,0:T(8,128)(2,1)S(1)} %get-tuple-element.9, bf16[3,2048,128]{2,1,0:T(8,128)(2,1)S(1)} %get-tuple-element.8, bf16[3,2048,128]{2,1,0:T(8,128)(2,1)S(1)} %copy-done.2, bf16[3,2048,128]{2,1,0:T(8,128)(2,1)S(1)} %get-tuple-element.23), kind=kOutput, calls=%fused_computation.84 | convolution fusion | flops 832077824 | bytes 7995392 | tf_op jit(solution)/shard_map/dot_general | solution.py:44
  21.5 1.1 %fusion.68 = f32[128,256]{1,0:T(8,128)S(1)} fusion(bf16[3,2048,128]{2,1,0:T(8,128)(2,1)S(1)} %get-tuple-element.20, bf16[3,2048,128]{2,1,0:T(8,128)(2,1)S(1)} %get-tuple-element.21, bf16[3,2048,128]{2,1,0:T(8,128)(2,1)S(1)} %get-tuple-element.22, bf16[3,2048,128]{2,1,0:T(8,128)(2,1)S(1)} %copy-done.2, bf16[3,2048,128]{2,1,0:T(8,128)(2,1)S(1)} %get-tuple-element.23), kind=kOutput, calls=%fused_computation.85 | convolution fusion | flops 832077824 | bytes 7995392 | tf_op jit(solution)/shard_map/dot_general | solution.py:44
  22.7 2.0 %fusion.150 = (f32[2048]{0:T(1024)S(1)}, f32[2048]{0:T(1024)S(1)}) fusion(s32[]{:T(128)} %bitcast.4, s32[]{:T(128)} %bitcast.3, s32[]{:T(128)S(6)} %mul.324, s32[]{:T(128)} %bitcast.2), kind=kLoop, calls=%fused_computation.233 | loop fusion | flops 153600 | bytes 16400 | tf_op jit(solution)/shard_map/sin | solution.py:32
  24.6 1.9 %fusion.144 = (f32[2048]{0:T(1024)S(1)}, f32[2048]{0:T(1024)S(1)}) fusion(s32[]{:T(128)} %bitcast.25, s32[]{:T(128)} %bitcast.24, s32[]{:T(128)S(6)} %mul.324, s32[]{:T(128)} %bitcast.23), kind=kLoop, calls=%fused_computation.227 | loop fusion | flops 153600 | bytes 16400 | tf_op jit(solution)/shard_map/sin | solution.py:32
  26.6 3.3 %fusion.47 = (bf16[3,2048,128]{2,1,0:T(8,128)(2,1)S(1)}, bf16[3,2048,128]{2,1,0:T(8,128)(2,1)S(1)}, bf16[3,2048,128]{2,1,0:T(8,128)(2,1)S(1)}, bf16[3,2048,128]{...) fusion(f32[2048]{0:T(1024)S(1)} %get-tuple-element.45, ...), kind=kLoop, calls=%fused_computation.70 | loop fusion | flops 17301504 | bytes 12615680 | tf_op jit(solution)/shard_map/convert.22
  29.9 1.1 %fusion.71 = f32[128,256]{1,0:T(8,128)S(1)} fusion(bf16[3,2048,128]{2,1,0:T(8,128)(2,1)S(1)} %get-tuple-element.17, bf16[3,2048,128]{2,1,0:T(8,128)(2,1)S(1)} %get-tuple-element.18, bf16[3,2048,128]{2,1,0:T(8,128)(2,1)S(1)} %get-tuple-element.19, bf16[3,2048,128]{2,1,0:T(8,128)(2,1)S(1)} %copy-done.2, bf16[3,2048,128]{2,1,0:T(8,128)(2,1)S(1)} %get-tuple-element.23), kind=kOutput, calls=%fused_computation.86 | convolution fusion | flops 832077824 | bytes 7995392 | tf_op jit(solution)/shard_map/dot_general | solution.py:44
  31.0 1.1 %fusion.62 = f32[128,256]{1,0:T(8,128)S(1)} fusion(bf16[3,2048,128]{2,1,0:T(8,128)(2,1)S(1)} %get-tuple-element.7, bf16[3,2048,128]{2,1,0:T(8,128)(2,1)S(1)} %get-tuple-element.6, bf16[3,2048,128]{2,1,0:T(8,128)(2,1)S(1)} %get-tuple-element.5, bf16[3,2048,128]{2,1,0:T(8,128)(2,1)S(1)} %copy-done.2, bf16[3,2048,128]{2,1,0:T(8,128)(2,1)S(1)} %get-tuple-element.23), kind=kOutput, calls=%fused_computation.83 | convolution fusion | flops 832077824 | bytes 7995392 | tf_op jit(solution)/shard_map/dot_general | solution.py:44
  32.2 0.8 pad_maximum_fusion.1
  33.8 0.7 gather_fusion.1
  34.6 23.0 %reduce-scatter.2.cloned.1.call-done = f32[4,2,32,128]{3,2,1,0:T(8,128)} async-done(((f32[4,2,128,128]{3,2,1,0:T(8,128)}), f32[4,2,32,128]{3,2,1,0:T(8,128)}) %reduce-scatter.2.cloned.1.call-update) | async-done | bytes 131088 | tf_op jit(solution)/shard_map/reduce_scatter | solution.py:83
  57.6 1.5 %gather_fusion = f32[16,2,32,128]{3,2,1,0:T(8,128)S(1)} fusion(f32[4,2,32,128]{3,2,1,0:T(8,128)} %reduce-scatter.2.cloned.1.call-done, s32[1024]{0:T(1024)S(1)} %pad_clamp_fusion.1), kind=kCustom, calls=%fused_computation | custom fusion | bytes 1048640 | tf_op jit(solution)/shard_map/gather | solution.py:87
  59.1 0.5 fusion.75
  59.6 0.5 fusion.74
  60.1 0.8 fusion.78
  60.9 19.0 %psum.7 = f32[2,32,128]{2,1,0:T(8,128)S(1)} all-reduce(f32[2,32,128]{2,1,0:T(8,128)S(1)} %fusion.78), channel_id=1, replica_groups=mesh['grp'=2,'ta'=4,'gx'=4] {'ta'}, use_global_device_ids=true, to_apply=%region_1.2 | all-reduce | flops 8192 | bytes 65536 | tf_op jit(solution)/shard_map/psum | solution.py:16
  80.0 5.4 %all_gather.3 = f32[2,128,128]{2,1,0:T(8,128)S(1)} all-gather(f32[2,32,128]{2,1,0:T(8,128)S(1)} %psum.7), channel_id=1, replica_groups=mesh['grp'=2,'ta'=4,'gx'=4] {'gx'}, dimensions={1}, use_global_device_ids=true | all-gather | bytes 163840 | tf_op jit(solution)/shard_map/all_gather | solution.py:85
  86.6 0.5 convolution_add_fusion.1
  88.0 11.2 %all_to_all.15 = f32[16,2,32,128]{3,2,1,0:T(8,128)S(1)} all-to-all(f32[16,2,32,128]{3,2,1,0:T(8,128)S(1)} %copy.25), channel_id=1, replica_groups=mesh['grp'=2,'ta'=4,'gx'=4] {'gx'}, dimensions={0} | all-to-all | bytes 1048576 | tf_op jit(solution)/shard_map/all_to_all | solution.py:89
  99.2 0.8 copy.26
  (31 shorter events, 2.2 us)
Async XLA Ops:
  6.5 27.3 %copy-start = (bf16[1,16,2,128,128]{4,3,2,1,0:T(8,128)(2,1)S(1)}, bf16[1,16,2,128,128]{4,3,2,1,0:T(8,128)(2,1)}, u32[]{:S(2)}) copy-start(bf16[1,16,2,128,128]{4,3,2,1,0:T(8,128)(2,1)} %param.7) | copy-start | bytes 3145732
  6.5 51.1 %reduce-scatter.2.cloned.1.call-start = ((), (), s32[]{:S(2)}) async-start(), calls=%async_computation.2 | async-start | bytes 655360 | tf_op jit(solution)/shard_map/reduce_scatter | solution.py:83
  15.5 4.9 %copy-start.2 = (bf16[3,2048,128]{2,1,0:T(8,128)(2,1)S(1)}, bf16[3,2048,128]{2,1,0:T(8,128)(2,1)}, u32[]{:S(2)}) copy-start(bf16[3,2048,128]{2,1,0:T(8,128)(2,1)} %get-tuple-element.24) | copy-start | bytes 4718596
  21.5 5.1 %copy-start.1 = (bf16[1,2,3,2048,128]{4,3,2,1,0:T(8,128)(2,1)S(1)}, bf16[1,2,3,2048,128]{4,3,2,1,0:T(8,128)(2,1)}, u32[]{:S(2)}) copy-start(bf16[1,2,3,2048,128]{4,3,2,1,0:T(8,128)(2,1)} %param.6) | copy-start | bytes 9437188
  31.0 2.8 %copy-start.3 = (s32[16]{0:T(128)S(1)}, s32[16]{0:T(128)}, u32[]{:S(2)}) copy-start(s32[16]{0:T(128)} %param.10) | copy-start | bytes 196
  32.1 2.4 %copy-start.4 = (s32[16]{0:T(128)S(1)}, s32[16]{0:T(128)}, u32[]{:S(2)}) copy-start(s32[16]{0:T(128)} %param.9) | copy-start | bytes 196
Sparse Core Ops, SparseCore 0:
  33.2 24.3 reduce-scatter.1
where the time goes:
time: 107 us
  blocking collectives  35.7 us (33%)
  waiting for transfers between devices  23 us (21%)
  other arithmetic  17.6 us (16%)
  between operations  14.4 us (13%)
  local copies, waits for them, and re-layouts  8.24 us (8%)
  matrix products  7.97 us (7%)
    reduce_scatter x1, waiting for transfers between devices, body(): lax.psum_scatter(local_terms, 'gx', scatter_dimension=2, tiled=True)  23 us
    psum x1, blocking collectives, broadcast(): return lax.psum(jnp.where(mine, array, jnp.zeros_like(array)), axis)  19 us
    all_to_all x1, blocking collectives, body(): lax.all_to_all(corr_rows, 'gx', split_axis=0, concat_axis=2, tiled=True)  11.2 us
    another operation x2, other arithmetic  8.14 us
    sin x4, other arithmetic, elemental(): sin_part = jnp.sin(angle)[None, :, None]  7.76 us
    all_gather x1, blocking collectives, body(): source = lax.all_gather(source_part, 'gx', axis=1, tiled=True)  5.42 us
    dot_general x4, matrix products, elemental(): lax.dot_general(stacked, phased, (((0,), (0,)), ((), ())), preferred_elem...  4.43 us
    dot_general x8, matrix products, matmul_high(): return jnp.matmul(left, right, precision=lax.Precision.HIGHEST)  3.53 us
  transfers between devices with their start and end apart: 1, of which 1 were waited for; matrix products, arithmetic and copies ran while one was open for 1% of the time, Pallas kernels for 0%

commit v1 on v0

v1 whole, which is shorter than its diff:
```python
import functools
import math

import jax
import jax.numpy as jnp
from jax import lax
from jax.experimental import pallas as pl
from jax.experimental.pallas import tpu as pltpu
from jax.sharding import PartitionSpec as P

LY = 32
LZ = 32
SUB = 8
PACK = 16


def turn_part(product, extent):
    if extent & (extent - 1) == 0:
        wrapped = jnp.bitwise_and(product, extent - 1)
    else:
        wrapped = jnp.mod(product, extent)
    return wrapped.astype(jnp.float32) / extent


def phase_tables(momenta_ref, m, first_x, sites, extent_x):
    shape = (SUB, sites // SUB)
    site = lax.broadcasted_iota(jnp.int32, shape, 1) * SUB + lax.broadcasted_iota(
        jnp.int32, shape, 0
    )
    coord_x = first_x + site // (LY * LZ)
    coord_y = site // LZ % LY
    coord_z = site % LZ
    turns = (
        turn_part(momenta_ref[m, 0] * coord_x, extent_x)
        + turn_part(momenta_ref[m, 1] * coord_y, LY)
        + turn_part(momenta_ref[m, 2] * coord_z, LZ)
    )
    angle = (2.0 * math.pi) * (turns - jnp.floor(turns + 0.5))
    return jnp.cos(angle), jnp.sin(angle)


def elemental_kernel(
    first, count, extent_x, scale, momenta_ref, place_ref, vec_ref, keep_ref, send_ref,
    left, phased, total
):
    color = pl.program_id(0)
    sites = vec_ref.shape[2]
    rank = vec_ref.shape[3]
    left[:rank] = vec_ref[0, 0].T
    left[rank:] = vec_ref[1, 0].T
    for k in range(count):
        cos_tab, sin_tab = phase_tables(momenta_ref, first + k, place_ref[0], sites, extent_x)
        for i in range(sites // PACK):
            rows = slice(i * PACK, (i + 1) * PACK)
            real = vec_ref[0, 0, rows, :].astype(jnp.float32)
            imag = vec_ref[1, 0, rows, :].astype(jnp.float32)

            def spread(table):
                return jnp.concatenate(
                    [
                        jnp.broadcast_to(table[:, 2 * i + h : 2 * i + h + 1], (SUB, rank))
                        for h in range(PACK // SUB)
                    ],
                    axis=0,
                )

            c = spread(cos_tab)
            s = spread(sin_tab)
            phased[k, rows, :rank] = (real * c + imag * s).astype(jnp.bfloat16)
            phased[k, rows, rank:] = (imag * c - real * s).astype(jnp.bfloat16)
        part = jnp.dot(left[...], phased[k], preferred_element_type=jnp.float32)

        @pl.when(color == 0)
        def _():
            total[k] = part

        @pl.when(color > 0)
        def _():
            total[k] = total[k] + part

    @pl.when(color == pl.num_programs(0) - 1)
    def _():
        odd = place_ref[1] == 1
        for k in range(count):
            re = (total[k, :rank, :rank] + total[k, rank:, rank:]) * scale
            im = (total[k, :rank, rank:] - total[k, rank:, :rank]) * scale
            keep_ref[k] = jnp.where(odd, im, re)
            send_ref[k] = jnp.where(odd, re, im)


def elementals(momenta, place, vectors, first, count, extent_x, scale):
    _, colors, sites, rank = vectors.shape
    out = jax.ShapeDtypeStruct((count, rank, rank), jnp.float32)
    smem = pl.BlockSpec(memory_space=pltpu.SMEM)
    return pl.pallas_call(
        functools.partial(elemental_kernel, first, count, extent_x, scale),
        grid=(colors,),
        in_specs=[smem, smem, pl.BlockSpec((2, 1, sites, rank), lambda c: (0, c, 0, 0))],
        out_specs=[pl.BlockSpec(memory_space=pltpu.VMEM)] * 2,
        out_shape=[out, out],
        scratch_shapes=[
            pltpu.VMEM((2 * rank, sites), jnp.bfloat16),
            pltpu.VMEM((count, sites, 2 * rank), jnp.bfloat16),
            pltpu.VMEM((count, 2 * rank, 2 * rank), jnp.float32),
        ],
        name="elementals",
    )(momenta, place, vectors)


def split_two(x):
    high = x.astype(jnp.bfloat16)
    return high, (x - high.astype(jnp.float32)).astype(jnp.bfloat16)


def bdot(a, b):
    return jnp.dot(a, b, preferred_element_type=jnp.float32)


def sink_kernel(spins, place_ref, mom_ref, pick_ref, mine0, other0, mine1, other1, per_ref, high_ref, low_ref):
    rank = per_ref.shape[-1]
    odd = place_ref[1] == 1
    start = place_ref[2]
    for j in range(spins):
        m = mom_ref[start + j]
        q = pick_ref[start + j]
        rest = jnp.maximum(m - 1, 0)
        mine = jnp.where(m == 0, mine0[0], mine1[rest])
        other = jnp.where(m == 0, other0[0], other1[rest])
        re_h, re_l = split_two(jnp.where(odd, other, mine))
        im_h, im_l = split_two(jnp.where(odd, mine, other))
        weights = jnp.concatenate([per_ref[q, 0], per_ref[q, 1]], axis=1)
        from_re = bdot(re_h, weights) + bdot(re_l, weights)
        from_im = bdot(im_h, weights) + bdot(im_l, weights)
        out_re = from_re[:, :rank] - from_im[:, rank:]
        out_im = from_re[:, rank:] + from_im[:, :rank]
        high_ref[j, 0], low_ref[j, 0] = split_two(out_re)
        high_ref[j, 1], low_ref[j, 1] = split_two(out_im)


def corr_kernel(scale, place_ref, high_ref, low_ref, mine_ref, other_ref, out_ref):
    spins, _, rank, _ = high_ref.shape
    odd = place_ref[1] == 1
    mine = mine_ref[0]
    other = other_ref[0]
    re_h, re_l = split_two(jnp.where(odd, other, mine))
    im_h, im_l = split_two(jnp.where(odd, mine, other))
    w_h = jnp.concatenate([re_h, im_h], axis=1)
    w_l = jnp.concatenate([re_l, im_l], axis=1)
    for j in range(spins):
        high = high_ref[j].reshape(2 * rank, rank)
        low = low_ref[j].reshape(2 * rank, rank)
        full = bdot(high, w_h) + (bdot(high, w_l) + bdot(low, w_h))
        out_ref[0, j, 0] = (full[:rank, :rank] - full[rank:, rank:]) * scale
        out_ref[0, j, 1] = (full[:rank, rank:] + full[rank:, :rank]) * scale


def swap(array, axis, bit):
    return lax.ppermute(array, axis, [(i, i ^ bit) for i in range(lax.axis_size(axis))])


def bits(size):
    return [1 << k for k in range((size - 1).bit_length())]


def chip_sum(keep, send):
    total = keep + swap(send, "gx", 1)
    for bit in bits(lax.axis_size("gx"))[1:]:
        total = total + swap(total, "gx", bit)
    return total


def body(vectors, peramb, momenta, sink_mom, spin_pick, src_time):
    vectors = vectors[0]
    peramb = peramb[0]
    _, colors, sites, rank = vectors.shape
    groups = lax.axis_size("gx")
    slab_x = sites // (LY * LZ)
    extent_x = slab_x * groups
    me = lax.axis_index("gx")
    spins = sink_mom.shape[0] // groups
    place = jnp.stack([me * slab_x, me % 2, me * spins]).astype(jnp.int32)
    scale = 1.0 / math.sqrt(colors * sites * groups)
    count = momenta.shape[0]
    run = functools.partial(
        elementals, momenta, place, vectors, extent_x=extent_x, scale=scale
    )
    slices = lax.axis_size("ta")
    root = jnp.mod(src_time[0], slices)
    apart = jnp.bitwise_xor(root, lax.axis_index("ta"))

    mine0 = chip_sum(*run(first=0, count=1))
    mine1 = chip_sum(*run(first=1, count=count - 1))
    source = mine0
    for bit in bits(slices):
        source = jnp.where(jnp.bitwise_and(apart, bit) != 0, swap(source, "ta", bit), source)
    source_other = swap(source, "gx", 1)
    other0 = swap(mine0, "gx", 1)
    other1 = swap(mine1, "gx", 1)

    smem = pl.BlockSpec(memory_space=pltpu.SMEM)
    vmem = pl.BlockSpec(memory_space=pltpu.VMEM)
    pair = jax.ShapeDtypeStruct((spins, 2, rank, rank), jnp.bfloat16)
    high, low = pl.pallas_call(
        functools.partial(sink_kernel, spins),
        in_specs=[smem] * 3 + [vmem] * 5,
        out_specs=[vmem] * 2,
        out_shape=[pair, pair],
        name="sink",
    )(place, sink_mom, spin_pick, mine0, other0, mine1, other1, peramb)
    return pl.pallas_call(
        functools.partial(corr_kernel, 1.0 / math.sqrt(rank)),
        in_specs=[smem] + [vmem] * 4,
        out_specs=vmem,
        out_shape=jax.ShapeDtypeStruct((1, spins, 2, rank, rank), jnp.float32),
        name="corr",
    )(place, high, low, source, source_other)


def solution(mesh):
    placed = (
        P(("grp", "ta"), None, None, "gx", None),
        P(("grp", "ta"), None, None, None, None),
        P("grp", None),
        P("grp"),
        P("grp"),
        P("grp"),
    )
    return jax.shard_map(
        body,
        mesh=mesh,
        in_specs=placed,
        out_specs=P(("grp", "ta"), "gx", None, None, None),
        check_vma=False,
    )
```

time: 107 us -> 46.4 us (0.43)
  blocking collectives: 35.7 us -> 0 us
  Pallas kernels: 0 us -> 27 us
  waiting for transfers between devices: 23 us -> 5.47 us
  other arithmetic: 17.6 us -> 1.62 us
  between operations: 14.4 us -> 0.81 us
  starting transfers between devices: 0.01 us -> 10 us
  matrix products: 7.97 us -> 0 us
  local copies, waits for them, and re-layouts: 8.24 us -> 1.33 us
    pallas_call x0 -> x4, Pallas kernels: none -> 27 us  [the longest x2 21.8 us: elementals(): pl.pallas_call(functools.partial(elemental_kernel, first, count, extent_x...]
    reduce_scatter x1 -> x0, waiting for transfers between devices: 23 us -> none  [body(): lax.psum_scatter(local_terms, 'gx', scatter_dimension=2, tiled=True)]
    psum x1 -> x0, blocking collectives: 19 us -> none  [broadcast(): return lax.psum(jnp.where(mine, array, jnp.zeros_like(array)), axis)]
    all_to_all x1 -> x0, blocking collectives: 11.2 us -> none  [body(): lax.all_to_all(corr_rows, 'gx', split_axis=0, concat_axis=2, tiled=True)]
    ppermute x0 -> x9, starting transfers between devices: none -> 10 us  [swap(): lax.ppermute(array, axis, [(i, i ^ bit) for i in range(lax.axis_size(axis...]
    another operation x7 -> x1, other arithmetic: 9.02 us -> 0.61 us  [body(): place = jnp.stack([me * slab_x, me % 2, me * spins]).astype(jnp.int32)]
    dot_general x12 -> x0, matrix products: 7.97 us -> none  [the longest x4 4.43 us: elemental(): lax.dot_general(stacked, phased, (((0,), (0,)), ((), ())), preferred_elem...]
    sin x4 -> x0, other arithmetic: 7.76 us -> none  [elemental(): sin_part = jnp.sin(angle)[None, :, None]]
  transfers between devices with their start and end apart: 1 -> 9, of which waited for: 1 -> 3; matrix products, arithmetic and copies ran while one was open for 1% -> 2% of each run, Pallas kernels for 0% -> 39%
where the time goes in v1:
time: 46.4 us; the launch traced here: 46.2 us
  Pallas kernels  27 us (58%)
  starting transfers between devices  10 us (22%)
  waiting for transfers between devices  5.47 us (12%)
  other arithmetic  1.62 us (3%)
  local copies, waits for them, and re-layouts  1.33 us (3%)
  between operations  0.81 us (2%)
    pallas_call x2, Pallas kernels, elementals(): pl.pallas_call(functools.partial(elemental_kernel, first, count, extent_x...  21.8 us
    ppermute x9, starting transfers between devices, swap(): lax.ppermute(array, axis, [(i, i ^ bit) for i in range(lax.axis_size(axis...  10 us
    ppermute x9, waiting for transfers between devices, swap(): lax.ppermute(array, axis, [(i, i ^ bit) for i in range(lax.axis_size(axis...  5.47 us
    pallas_call x1, Pallas kernels, body(): pl.pallas_call(functools.partial(sink_kernel, spins), in_specs=[smem] * 3...  2.74 us
    pallas_call x1, Pallas kernels, body(): pl.pallas_call(functools.partial(corr_kernel, 1.0 / math.sqrt(rank)), in_...  2.39 us
    unnamed x14, local copies, waits for them, and re-layouts  1.33 us
    add x2, other arithmetic, chip_sum(): total = keep + swap(send, 'gx', 1)  0.96 us
  transfers between devices with their start and end apart: 9, of which 3 were waited for; matrix products, arithmetic and copies ran while one was open for 2% of the time, Pallas kernels for 39%

profile of v1, /device:TPU:0, one launch (start us, length us, event | category | flops | bytes accessed | tf_op | source)
XLA Modules:
  0.0 46.2 jit_solution(774356035113648932)
XLA Ops:
  0.0 0.6 %pad_add_fusion.place_ref = s32[3]{0:T(128)} fusion(s32[1]{0:T(128)} %bitcast.2, s32[1]{0:T(128)} %bitcast.1, s32[1]{0:T(128)} %bitcast), kind=kLoop, calls=%fused_computation.2 | loop fusion | flops 6 | bytes 24 | tf_op jit(solution)/shard_map/stack | solution.py:181
  0.6 6.7 %elementals.2 = (f32[1,128,128]{2,1,0:T(8,128)}, f32[1,128,128]{2,1,0:T(8,128)}) custom-call(s32[4,3]{1,0:T(4,128)} %momenta_ref.3, s32[3]{0:T(128)} %pad_add_fusion.place_ref, bf16[2,3,2048,128]{3,2,1,0:T(8,128)(2,1)} %bitcast.9), custom_call_target="tpu_custom_call" | custom-call | tf_op jit(solution)/shard_map/elementals/pallas_call | solution.py:95
  7.3 0.5 %collective-permute-start = (f32[1,128,128]{2,1,0:T(8,128)}, f32[1,128,128]{2,1,0:T(8,128)S(1)}, u32[]{:S(2)}, u32[]{:S(2)}) collective-permute-start(f32[1,128,128]{2,1,0:T(8,128)} %get-tuple-element.12), channel_id=1, source_target_pairs={{0,1},{1,0},{2,3},{3,2},{4,5},{5,4},{6,7},{7,6},{8,9},{9,8},{10,11... | collective-permute-start | bytes 196616 | tf_op jit(solution)/shard_map/ppermute | solution.py:158
  7.8 15.1 %elementals.3 = (f32[3,128,128]{2,1,0:T(8,128)}, f32[3,128,128]{2,1,0:T(8,128)}) custom-call(s32[4,3]{1,0:T(4,128)} %momenta_ref.3, s32[3]{0:T(128)} %pad_add_fusion.place_ref, bf16[2,3,2048,128]{3,2,1,0:T(8,128)(2,1)} %bitcast.10), custom_call_target="tpu_custom_call" | custom-call | tf_op jit(solution)/shard_map/elementals/pallas_call | solution.py:95
  22.9 0.0 collective-permute-start.3
  23.0 0.0 collective-permute-done
  23.0 3.0 %collective-permute-start.1 = (f32[1,128,128]{2,1,0:T(8,128)S(1)}, f32[1,128,128]{2,1,0:T(8,128)S(1)}, u32[]{:S(2)}, u32[]{:S(2)}) collective-permute-start(f32[1,128,128]{2,1,0:T(8,128)S(1)} %add.20), channel_id=1, source_target_pairs={{0,2},{1,3},{2,0},{3,1},{4,6},{5,7},{6,4},{7,5},{8,10},{9,11},{10,... | collective-permute-start | bytes 196616 | tf_op jit(solution)/shard_map/ppermute | solution.py:158
  26.0 2.3 %collective-permute-done.1 = f32[1,128,128]{2,1,0:T(8,128)S(1)} collective-permute-done((f32[1,128,128]{2,1,0:T(8,128)S(1)}, f32[1,128,128]{2,1,0:T(8,128)S(1)}, u32[]{:S(2)}, u32[]{:S(2)}) %collective-permute-start.1) | collective-permute-done | bytes 65568 | tf_op jit(solution)/shard_map/ppermute | solution.py:158
  28.3 2.1 %collective-permute-start.6 = (f32[1,128,128]{2,1,0:T(8,128)S(1)}, f32[1,128,128]{2,1,0:T(8,128)S(1)}, u32[]{:S(2)}, u32[]{:S(2)}) collective-permute-start(f32[1,128,128]{2,1,0:T(8,128)S(1)} %add.21.mine0), channel_id=1, source_target_pairs={{0,4},{4,0},{8,12},{12,8},{1,5},{5,1},{9,13},{13,9},{2,6},{6,2},{1... | collective-permute-start | bytes 196616 | tf_op jit(solution)/shard_map/ppermute | solution.py:158
  31.1 0.0 collective-permute-done.3
  31.1 1.0 %add.22 = f32[3,128,128]{2,1,0:T(8,128)S(1)} add(f32[3,128,128]{2,1,0:T(8,128)} %get-tuple-element.13, f32[3,128,128]{2,1,0:T(8,128)S(1)} %collective-permute-done.3) | non-fusion elementwise | flops 49152 | bytes 589824 | tf_op jit(solution)/shard_map/add | solution.py:166
  32.1 1.6 %collective-permute-start.4 = (f32[3,128,128]{2,1,0:T(8,128)S(1)}, f32[3,128,128]{2,1,0:T(8,128)S(1)}, u32[]{:S(2)}, u32[]{:S(2)}) collective-permute-start(f32[3,128,128]{2,1,0:T(8,128)S(1)} %add.22), channel_id=1, source_target_pairs={{0,2},{1,3},{2,0},{3,1},{4,6},{5,7},{6,4},{7,5},{8,10},{9,11},{10,... | collective-permute-start | bytes 589832 | tf_op jit(solution)/shard_map/ppermute | solution.py:158
  33.6 0.0 collective-permute-done.6
  33.7 2.7 %collective-permute-start.7 = (f32[1,128,128]{2,1,0:T(8,128)S(1)}, f32[1,128,128]{2,1,0:T(8,128)S(1)}, u32[]{:S(2)}, u32[]{:S(2)}) collective-permute-start(f32[1,128,128]{2,1,0:T(8,128)S(1)} %broadcast_select_fusion), channel_id=1, source_target_pairs={{0,8},{4,12},{8,0},{12,4},{1,9},{5,13},{9,1},{13,5},{2,10},{6,14},... | collective-permute-start | bytes 196616 | tf_op jit(solution)/shard_map/ppermute | solution.py:158
  36.3 1.5 %collective-permute-done.4 = f32[3,128,128]{2,1,0:T(8,128)S(1)} collective-permute-done((f32[3,128,128]{2,1,0:T(8,128)S(1)}, f32[3,128,128]{2,1,0:T(8,128)S(1)}, u32[]{:S(2)}, u32[]{:S(2)}) %collective-permute-start.4) | collective-permute-done | bytes 196640 | tf_op jit(solution)/shard_map/ppermute | solution.py:158
  37.8 0.0 copy-start
  37.9 0.1 collective-permute-start.5
  37.9 1.6 %collective-permute-done.7 = f32[1,128,128]{2,1,0:T(8,128)S(1)} collective-permute-done((f32[1,128,128]{2,1,0:T(8,128)S(1)}, f32[1,128,128]{2,1,0:T(8,128)S(1)}, u32[]{:S(2)}, u32[]{:S(2)}) %collective-permute-start.7) | collective-permute-done | bytes 65568 | tf_op jit(solution)/shard_map/ppermute | solution.py:158
  39.6 0.1 collective-permute-start.8
  39.7 0.6 %copy-done.4 = f32[1,128,128]{2,1,0:T(8,128)} copy-done((f32[1,128,128]{2,1,0:T(8,128)}, f32[1,128,128]{2,1,0:T(8,128)S(1)}, u32[]{:S(2)}) %copy-start.4) | copy-done | bytes 65560
  40.3 0.1 copy-done.3
  40.4 2.7 %sink.1 = (bf16[4,2,128,128]{3,2,1,0:T(8,128)(2,1)}, bf16[4,2,128,128]{3,2,1,0:T(8,128)(2,1)}) custom-call(s32[3]{0:T(128)} %pad_add_fusion.place_ref, s32[16]{0:T(128)} %mom_ref.1, s32[16]{0:T(128)} %pick_ref.1, f32[1,128,128]{2,1,0:T(8,128)} %copy-done.1, f32[1,128,128]{2,1,0:T(8,128)} %copy-done.4, f32[3,128,128]{2,1,0:T(8,128)} %copy-done, ...), custom_call_target="tpu_custom_call" | custom-call | tf_op jit(solution)/shard_map/sink/pallas_call | solution.py:203
  43.2 0.6 %copy-done.5 = f32[1,128,128]{2,1,0:T(8,128)} copy-done((f32[1,128,128]{2,1,0:T(8,128)}, f32[1,128,128]{2,1,0:T(8,128)S(1)}, u32[]{:S(2)}) %copy-start.5) | copy-done | bytes 65560
  43.8 2.4 %corr.1 = f32[1,4,2,128,128]{4,3,2,1,0:T(8,128)} custom-call(s32[3]{0:T(128)} %pad_add_fusion.place_ref, bf16[4,2,128,128]{3,2,1,0:T(8,128)(2,1)} %get-tuple-element.15.high_ref, bf16[4,2,128,128]{3,2,1,0:T(8,128)(2,1)} %get-tuple-element.16.low_ref, f32[1,128,128]{2,1,0:T(8,128)} %copy-done.2, f32[1,128,128]{2,1,0:T(8,128)} %copy-done.5), custom_call_target="tpu_custom_call" | custom-call | tf_op jit(solution)/shard_map/corr/pallas_call | solution.py:210
  (19 shorter events, 0.1 us)
Async XLA Ops:
  7.3 15.7 %copy-start.6 = (f32[1,128,128]{2,1,0:T(8,128)S(1)}, f32[1,128,128]{2,1,0:T(8,128)}, u32[]{:S(2)}) copy-start(f32[1,128,128]{2,1,0:T(8,128)} %get-tuple-element.11) | copy-start | bytes 196612
  7.3 15.7 %collective-permute-start = (f32[1,128,128]{2,1,0:T(8,128)}, f32[1,128,128]{2,1,0:T(8,128)S(1)}, u32[]{:S(2)}, u32[]{:S(2)}) collective-permute-start(f32[1,128,128]{2,1,0:T(8,128)} %get-tuple-element.12), channel_id=1, source_target_pairs={{0,1},{1,0},{2,3},{3,2},{4,5},{5,4},{6,7},{7,6},{8,9},{9,8},{10,11... | collective-permute-start | bytes 196616 | tf_op jit(solution)/shard_map/ppermute | solution.py:158
  22.9 8.2 %collective-permute-start.3 = (f32[3,128,128]{2,1,0:T(8,128)}, f32[3,128,128]{2,1,0:T(8,128)S(1)}, u32[]{:S(2)}, u32[]{:S(2)}) collective-permute-start(f32[3,128,128]{2,1,0:T(8,128)} %get-tuple-element.14), channel_id=1, source_target_pairs={{0,1},{1,0},{2,3},{3,2},{4,5},{5,4},{6,7},{7,6},{8,9},{9,8},{10,11... | collective-permute-start | bytes 589832 | tf_op jit(solution)/shard_map/ppermute | solution.py:158
  23.0 5.3 %collective-permute-start.1 = (f32[1,128,128]{2,1,0:T(8,128)S(1)}, f32[1,128,128]{2,1,0:T(8,128)S(1)}, u32[]{:S(2)}, u32[]{:S(2)}) collective-permute-start(f32[1,128,128]{2,1,0:T(8,128)S(1)} %add.20), channel_id=1, source_target_pairs={{0,2},{1,3},{2,0},{3,1},{4,6},{5,7},{6,4},{7,5},{8,10},{9,11},{10,... | collective-permute-start | bytes 196616 | tf_op jit(solution)/shard_map/ppermute | solution.py:158
  28.3 11.4 %copy-start.1 = (f32[1,128,128]{2,1,0:T(8,128)}, f32[1,128,128]{2,1,0:T(8,128)S(1)}, u32[]{:S(2)}) copy-start(f32[1,128,128]{2,1,0:T(8,128)S(1)} %add.21.mine0) | copy-start | bytes 196612
  28.3 5.3 %collective-permute-start.6 = (f32[1,128,128]{2,1,0:T(8,128)S(1)}, f32[1,128,128]{2,1,0:T(8,128)S(1)}, u32[]{:S(2)}, u32[]{:S(2)}) collective-permute-start(f32[1,128,128]{2,1,0:T(8,128)S(1)} %add.21.mine0), channel_id=1, source_target_pairs={{0,4},{4,0},{8,12},{12,8},{1,5},{5,1},{9,13},{13,9},{2,6},{6,2},{1... | collective-permute-start | bytes 196616 | tf_op jit(solution)/shard_map/ppermute | solution.py:158
  32.1 5.7 %collective-permute-start.4 = (f32[3,128,128]{2,1,0:T(8,128)S(1)}, f32[3,128,128]{2,1,0:T(8,128)S(1)}, u32[]{:S(2)}, u32[]{:S(2)}) collective-permute-start(f32[3,128,128]{2,1,0:T(8,128)S(1)} %add.22), channel_id=1, source_target_pairs={{0,2},{1,3},{2,0},{3,1},{4,6},{5,7},{6,4},{7,5},{8,10},{9,11},{10,... | collective-permute-start | bytes 589832 | tf_op jit(solution)/shard_map/ppermute | solution.py:158
  33.7 5.9 %collective-permute-start.7 = (f32[1,128,128]{2,1,0:T(8,128)S(1)}, f32[1,128,128]{2,1,0:T(8,128)S(1)}, u32[]{:S(2)}, u32[]{:S(2)}) collective-permute-start(f32[1,128,128]{2,1,0:T(8,128)S(1)} %broadcast_select_fusion), channel_id=1, source_target_pairs={{0,8},{4,12},{8,0},{12,4},{1,9},{5,13},{9,1},{13,5},{2,10},{6,14},... | collective-permute-start | bytes 196616 | tf_op jit(solution)/shard_map/ppermute | solution.py:158
  36.3 3.4 %collective-permute-start.2 = (f32[1,128,128]{2,1,0:T(8,128)S(1)}, f32[1,128,128]{2,1,0:T(8,128)S(1)}, u32[]{:S(2)}, u32[]{:S(2)}) collective-permute-start(f32[1,128,128]{2,1,0:T(8,128)S(1)} %add.21.mine0), channel_id=1, source_target_pairs={{0,1},{1,0},{2,3},{3,2},{4,5},{5,4},{6,7},{7,6},{8,9},{9,8},{10,11... | collective-permute-start | bytes 196616 | tf_op jit(solution)/shard_map/ppermute | solution.py:158
  37.8 1.9 %copy-start = (f32[3,128,128]{2,1,0:T(8,128)}, f32[3,128,128]{2,1,0:T(8,128)S(1)}, u32[]{:S(2)}) copy-start(f32[3,128,128]{2,1,0:T(8,128)S(1)} %add.23.mine1) | copy-start | bytes 589828
  37.9 1.9 %collective-permute-start.5 = (f32[3,128,128]{2,1,0:T(8,128)S(1)}, f32[3,128,128]{2,1,0:T(8,128)S(1)}, u32[]{:S(2)}, u32[]{:S(2)}) collective-permute-start(f32[3,128,128]{2,1,0:T(8,128)S(1)} %add.23.mine1), channel_id=1, source_target_pairs={{0,1},{1,0},{2,3},{3,2},{4,5},{5,4},{6,7},{7,6},{8,9},{9,8},{10,11... | collective-permute-start | bytes 589832 | tf_op jit(solution)/shard_map/ppermute | solution.py:158
  39.6 3.6 %copy-start.2 = (f32[1,128,128]{2,1,0:T(8,128)}, f32[1,128,128]{2,1,0:T(8,128)S(1)}, u32[]{:S(2)}) copy-start(f32[1,128,128]{2,1,0:T(8,128)S(1)} %broadcast_select_fusion.1.mine_ref) | copy-start | bytes 196612
  39.6 3.6 %collective-permute-start.8 = (f32[1,128,128]{2,1,0:T(8,128)S(1)}, f32[1,128,128]{2,1,0:T(8,128)S(1)}, u32[]{:S(2)}, u32[]{:S(2)}) collective-permute-start(f32[1,128,128]{2,1,0:T(8,128)S(1)} %broadcast_select_fusion.1.mine_ref), channel_id=1, source_target_pairs={{0,1},{1,0},{2,3},{3,2},{4,5},{5,4},{6,7},{7,6},{8,9},{9,8},{10,11... | collective-permute-start | bytes 196616 | tf_op jit(solution)/shard_map/ppermute | solution.py:158
  39.7 0.6 %copy-start.4 = (f32[1,128,128]{2,1,0:T(8,128)}, f32[1,128,128]{2,1,0:T(8,128)S(1)}, u32[]{:S(2)}) copy-start(f32[1,128,128]{2,1,0:T(8,128)S(1)} %collective-permute-done.2.other0) | copy-start | bytes 196612
  39.7 0.7 %copy-start.3 = (f32[3,128,128]{2,1,0:T(8,128)}, f32[3,128,128]{2,1,0:T(8,128)S(1)}, u32[]{:S(2)}) copy-start(f32[3,128,128]{2,1,0:T(8,128)S(1)} %collective-permute-done.5.other1) | copy-start | bytes 589828
  43.2 0.6 %copy-start.5 = (f32[1,128,128]{2,1,0:T(8,128)}, f32[1,128,128]{2,1,0:T(8,128)S(1)}, u32[]{:S(2)}) copy-start(f32[1,128,128]{2,1,0:T(8,128)S(1)} %collective-permute-done.8.other_ref) | copy-start | bytes 196612
